TPU v7x, 32 devices: a whole 2x2x4 slice. The times are simulated.
32 devices in a mesh: dp: 4 (over x, core), fsdp: 8 (over z, y).
Axes of the slice: x: 2, y: 2, z: 4, core: 2. Of those that a mesh axis runs over, the one named last changes fastest.
Arguments:
- tokens: bfloat16 [4, 1024, 768], P('dp', 'fsdp'), may hold values from -6 to 6
- ln1_gain: bfloat16 [768], P('fsdp'), may hold values from 0.099609375 to 1.8984375
- ln1_bias: bfloat16 [768], P('fsdp'), may hold values from -1.75 to 1.75
- ln2_gain: bfloat16 [768], P('fsdp'), may hold values from 0.099609375 to 1.8984375
- ln2_bias: bfloat16 [768], P('fsdp'), may hold values from -1.75 to 1.75
- qkv_weight: bfloat16 [768, 2304], P('fsdp'), may hold values from -0.21875 to 0.21875
- qkv_bias: bfloat16 [2304], P('fsdp'), may hold values from -3 to 3
- out_weight: bfloat16 [768, 768], P('fsdp'), may hold values from -1.75 to 1.75
- out_bias: bfloat16 [768], P('fsdp'), may hold values from -3 to 3
- up_weight: bfloat16 [768, 3072], P('fsdp'), may hold values from -0.21875 to 0.21875
- up_bias: bfloat16 [3072], P('fsdp'), may hold values from -3 to 3
- down_weight: bfloat16 [3072, 768], P('fsdp'), may hold values from -0.109375 to 0.109375
- down_bias: bfloat16 [768], P('fsdp'), may hold values from -3 to 3
- cotangent: bfloat16 [4, 1024, 768], P('dp', 'fsdp'), may hold values from -6 to 6
Outputs:
- layer_output: bfloat16 [4, 1024, 768], P('dp', 'fsdp')
- input_grad: float32 [4, 1024, 768], P('dp', 'fsdp')
- grad_ln1_gain: float32 [768], P('fsdp')
- grad_ln1_bias: float32 [768], P('fsdp')
- grad_ln2_gain: float32 [768], P('fsdp')
- grad_ln2_bias: float32 [768], P('fsdp')
- grad_qkv_weight: float32 [768, 2304], P('fsdp')
- grad_qkv_bias: float32 [2304], P('fsdp')
- grad_out_weight: float32 [768, 768], P('fsdp')
- grad_out_bias: float32 [768], P('fsdp')
- grad_up_weight: float32 [768, 3072], P('fsdp')
- grad_up_bias: float32 [3072], P('fsdp')
- grad_down_weight: float32 [3072, 768], P('fsdp')
- grad_down_bias: float32 [768], P('fsdp')
All inputs are finite; a program needn't handle non-finite values.
Results may differ from a plain program's by a relative error of at most 0.018.
Values may be sent and summed in bfloat16 or wider, within the bound.
A program may use at most 128 MiB of HBM per device.

v0:
```python
import math

import jax
import jax.numpy as jnp
from jax import lax
from jax.sharding import PartitionSpec as P

D = 768
HEADS = 12
HEAD = 64
ROT = 16


epsilon = 1e-05
inv_root_two = 1.0 / math.sqrt(2.0)
inv_root_twopi = 1.0 / math.sqrt(2.0 * math.pi)


def layer_norm(inputs, gain, shift):
    center = inputs - jnp.mean(inputs, axis=-1, keepdims=True)
    inverse = lax.rsqrt(jnp.mean(center * center, axis=-1, keepdims=True) + epsilon)
    normed = center * inverse
    return (normed * gain + shift, normed, inverse)


def norm_back(grad_norm, normed, inverse, gain):
    scaled = grad_norm * gain
    return inverse * (
        scaled
        - jnp.mean(scaled, axis=-1, keepdims=True)
        - normed * jnp.mean(scaled * normed, axis=-1, keepdims=True)
    )


def angles(places):
    half = ROT // 2
    inverse = 10000.0 ** (-(jnp.arange(half, dtype=jnp.float32) * 2.0) / ROT)
    angle = places[:, None] * inverse[None, :]
    return (jnp.cos(angle)[:, None, :], jnp.sin(angle)[:, None, :])


def rotary(tensor, cosine, sine, direction):
    half = ROT // 2
    first = tensor[..., :half]
    second = tensor[..., half:ROT]
    return jnp.concatenate(
        [
            first * cosine - direction * second * sine,
            second * cosine + direction * first * sine,
            tensor[..., ROT:],
        ],
        axis=-1,
    )


def block_scores(queries, keys_all, number, span, rank_here, rows):
    key_block = lax.dynamic_slice_in_dim(keys_all, number * span, span, 0).reshape(
        span, HEADS, HEAD
    )
    scores = jnp.einsum("qhd,khd->hqk", queries, key_block, preferred_element_type=jnp.float32)
    key_places = number * span + jnp.arange(span, dtype=jnp.int32)
    query_places = rank_here * rows + jnp.arange(rows, dtype=jnp.int32)
    visible = key_places[None, :] <= query_places[:, None]
    return (scores, visible[None], key_block)


def value_block(values_all, number, span):
    return lax.dynamic_slice_in_dim(values_all, number * span, span, 0).reshape(span, HEADS, HEAD)


def body(
    tokens,
    ln1_gain,
    ln1_bias,
    ln2_gain,
    ln2_bias,
    qkv_weight,
    qkv_bias,
    out_weight,
    out_bias,
    up_weight,
    up_bias,
    down_weight,
    down_bias,
    cotangent,
):
    rank_here = lax.axis_index("fsdp")
    count_dev = lax.axis_size("fsdp")
    gathered = (
        lax.all_gather(ln1_gain, "fsdp", axis=0, tiled=True),
        lax.all_gather(ln1_bias, "fsdp", axis=0, tiled=True),
        lax.all_gather(ln2_gain, "fsdp", axis=0, tiled=True),
        lax.all_gather(ln2_bias, "fsdp", axis=0, tiled=True),
        lax.all_gather(qkv_weight, "fsdp", axis=0, tiled=True),
        lax.all_gather(qkv_bias, "fsdp", axis=0, tiled=True),
        lax.all_gather(out_weight, "fsdp", axis=0, tiled=True),
        lax.all_gather(out_bias, "fsdp", axis=0, tiled=True),
        lax.all_gather(up_weight, "fsdp", axis=0, tiled=True),
        lax.all_gather(up_bias, "fsdp", axis=0, tiled=True),
        lax.all_gather(down_weight, "fsdp", axis=0, tiled=True),
        lax.all_gather(down_bias, "fsdp", axis=0, tiled=True),
    )
    (
        gain_first,
        bias_first,
        gain_second,
        bias_second,
        w_qkv,
        b_qkv,
        w_out,
        b_out,
        w_up,
        b_up,
        w_down,
        b_down,
    ) = gathered
    inputs = tokens[0].astype(jnp.float32)
    rows = inputs.shape[0]
    places = (rank_here * rows + jnp.arange(rows, dtype=jnp.int32)).astype(jnp.float32)
    cosine, sine = angles(places)
    first_h, normed_one, inverse_one = layer_norm(
        inputs, gain_first.astype(jnp.float32), bias_first.astype(jnp.float32)
    )
    second_h, normed_two, inverse_two = layer_norm(
        inputs, gain_second.astype(jnp.float32), bias_second.astype(jnp.float32)
    )
    first_low = first_h.astype(jnp.bfloat16)
    second_low = second_h.astype(jnp.bfloat16)
    projected = jnp.dot(first_low, w_qkv, preferred_element_type=jnp.float32) + b_qkv.astype(
        jnp.float32
    )
    queries = (
        rotary(projected[:, :D].reshape(rows, HEADS, HEAD), cosine, sine, 1.0) * 0.125
    ).astype(jnp.bfloat16)
    key_local = (
        rotary(projected[:, D : 2 * D].reshape(rows, HEADS, HEAD), cosine, sine, 1.0)
        .astype(jnp.bfloat16)
        .reshape(rows, D)
    )
    value_local = projected[:, 2 * D :].astype(jnp.bfloat16)
    keys_all, values_all = (
        lax.all_gather(key_local, "fsdp", axis=0, tiled=True),
        lax.all_gather(value_local, "fsdp", axis=0, tiled=True),
    )
    length = keys_all.shape[0]
    group = max(1, min(count_dev, 512 // rows))
    span = rows * group
    needed = rank_here // group + 1

    def stats_step(number, carry):
        run_max, run_total = carry
        scores, visible, key_block = block_scores(queries, keys_all, number, span, rank_here, rows)
        masked = jnp.where(visible, scores, -1e30)
        new_max = jnp.maximum(run_max, jnp.max(masked, axis=-1, keepdims=True))
        weights_now = jnp.where(visible, jnp.exp(masked - new_max), 0.0)
        run_total = run_total * jnp.exp(run_max - new_max) + jnp.sum(
            weights_now, axis=-1, keepdims=True
        )
        return (new_max, run_total)

    start_max = jnp.full((HEADS, rows, 1), -1e30, jnp.float32)
    start_total = jnp.zeros((HEADS, rows, 1), jnp.float32)
    run_max, run_total = lax.fori_loop(0, needed, stats_step, (start_max, start_total))
    log_total = run_max + jnp.log(run_total)

    def mix_step(number, accum):
        scores, visible, key_block = block_scores(queries, keys_all, number, span, rank_here, rows)
        probs = jnp.where(visible, jnp.exp(scores - log_total), 0.0).astype(jnp.bfloat16)
        return accum + jnp.einsum(
            "hqk,khd->qhd",
            probs,
            value_block(values_all, number, span),
            preferred_element_type=jnp.float32,
        )

    attended = lax.fori_loop(0, needed, mix_step, jnp.zeros((rows, HEADS, HEAD), jnp.float32))
    attended_low = attended.reshape(rows, D).astype(jnp.bfloat16)
    branch_attn = jnp.dot(attended_low, w_out, preferred_element_type=jnp.float32) + b_out.astype(
        jnp.float32
    )
    hidden_pre = jnp.dot(second_low, w_up, preferred_element_type=jnp.float32) + b_up.astype(
        jnp.float32
    )
    hidden_low = jax.nn.gelu(hidden_pre, approximate=False).astype(jnp.bfloat16)
    branch_mlp = jnp.dot(hidden_low, w_down, preferred_element_type=jnp.float32) + b_down.astype(
        jnp.float32
    )
    layer_output = (inputs + branch_attn + branch_mlp).astype(jnp.bfloat16)[None]
    again = (
        lax.all_gather(ln1_gain, "fsdp", axis=0, tiled=True),
        lax.all_gather(ln1_bias, "fsdp", axis=0, tiled=True),
        lax.all_gather(ln2_gain, "fsdp", axis=0, tiled=True),
        lax.all_gather(ln2_bias, "fsdp", axis=0, tiled=True),
        lax.all_gather(qkv_weight, "fsdp", axis=0, tiled=True),
        lax.all_gather(qkv_bias, "fsdp", axis=0, tiled=True),
        lax.all_gather(out_weight, "fsdp", axis=0, tiled=True),
        lax.all_gather(out_bias, "fsdp", axis=0, tiled=True),
        lax.all_gather(up_weight, "fsdp", axis=0, tiled=True),
        lax.all_gather(up_bias, "fsdp", axis=0, tiled=True),
        lax.all_gather(down_weight, "fsdp", axis=0, tiled=True),
        lax.all_gather(down_bias, "fsdp", axis=0, tiled=True),
    )
    gain_one_b = again[0].astype(jnp.float32)
    gain_two_b = again[2].astype(jnp.float32)
    w_qkv_b = again[4]
    w_out_b = again[6]
    w_up_b = again[8]
    w_down_b = again[10]
    grad_out = cotangent[0]
    grad_float = grad_out.astype(jnp.float32)
    bias_total = jnp.sum(grad_float, axis=0)
    grad_w_out = jnp.einsum("ti,to->io", attended_low, grad_out, preferred_element_type=jnp.float32)
    grad_w_down = jnp.einsum("tf,to->fo", hidden_low, grad_out, preferred_element_type=jnp.float32)
    grad_hidden = jnp.einsum("to,fo->tf", grad_out, w_down_b, preferred_element_type=jnp.float32)
    slope = (
        0.5 * (1.0 + lax.erf(hidden_pre * inv_root_two))
        + hidden_pre * jnp.exp(-0.5 * hidden_pre * hidden_pre) * inv_root_twopi
    )
    grad_pre = (grad_hidden * slope).astype(jnp.bfloat16)
    grad_w_up = jnp.einsum("ti,tf->if", second_low, grad_pre, preferred_element_type=jnp.float32)
    grad_b_up = jnp.sum(grad_pre.astype(jnp.float32), axis=0)
    grad_second = jnp.einsum("tf,if->ti", grad_pre, w_up_b, preferred_element_type=jnp.float32)
    grad_att = (
        jnp.einsum("to,io->ti", grad_out, w_out_b, preferred_element_type=jnp.float32)
        .astype(jnp.bfloat16)
        .reshape(rows, HEADS, HEAD)
    )
    delta = jnp.transpose(jnp.sum(grad_att.astype(jnp.float32) * attended, axis=-1))[:, :, None]
    keys_back, values_back = (
        lax.all_gather(key_local, "fsdp", axis=0, tiled=True),
        lax.all_gather(value_local, "fsdp", axis=0, tiled=True),
    )

    def grad_step(number, carry):
        grad_query, grad_keys, grad_values = carry
        scores, visible, key_block = block_scores(queries, keys_back, number, span, rank_here, rows)
        values_here = value_block(values_back, number, span)
        probs = jnp.where(visible, jnp.exp(scores - log_total), 0.0)
        grad_probs = jnp.einsum(
            "qhd,khd->hqk", grad_att, values_here, preferred_element_type=jnp.float32
        )
        grad_scores = (probs * (grad_probs - delta)).astype(jnp.bfloat16)
        grad_query = grad_query + jnp.einsum(
            "hqk,khd->qhd", grad_scores, key_block, preferred_element_type=jnp.float32
        )
        key_part = jnp.einsum(
            "hqk,qhd->khd", grad_scores, queries, preferred_element_type=jnp.float32
        )
        value_part = jnp.einsum(
            "hqk,qhd->khd", probs.astype(jnp.bfloat16), grad_att, preferred_element_type=jnp.float32
        )
        grad_keys = lax.dynamic_update_slice_in_dim(grad_keys, key_part, number * span, 0)
        grad_values = lax.dynamic_update_slice_in_dim(grad_values, value_part, number * span, 0)
        return (grad_query, grad_keys, grad_values)

    empty_keys = jnp.zeros((length, HEADS, HEAD), jnp.float32)
    grad_query, grad_keys, grad_values = lax.fori_loop(
        0, needed, grad_step, (jnp.zeros((rows, HEADS, HEAD), jnp.float32), empty_keys, empty_keys)
    )
    keys_mine, values_mine = (
        lax.psum_scatter(
            grad_keys.reshape(length, D).astype(jnp.bfloat16),
            "fsdp",
            scatter_dimension=0,
            tiled=True,
        ).astype(jnp.float32),
        lax.psum_scatter(
            grad_values.reshape(length, D).astype(jnp.bfloat16),
            "fsdp",
            scatter_dimension=0,
            tiled=True,
        ).astype(jnp.float32),
    )
    query_lin = rotary(grad_query * 0.125, cosine, sine, -1.0).reshape(rows, D)
    key_lin = rotary(keys_mine.reshape(rows, HEADS, HEAD), cosine, sine, -1.0).reshape(rows, D)
    grad_proj = jnp.concatenate([query_lin, key_lin, values_mine], axis=1).astype(jnp.bfloat16)
    grad_w_qkv = jnp.einsum("ti,tp->ip", first_low, grad_proj, preferred_element_type=jnp.float32)
    grad_b_qkv = jnp.sum(grad_proj.astype(jnp.float32), axis=0)
    grad_first = jnp.einsum("tp,ip->ti", grad_proj, w_qkv_b, preferred_element_type=jnp.float32)
    grad_gain_one = jnp.sum(grad_first * normed_one, axis=0)
    grad_bias_one = jnp.sum(grad_first, axis=0)
    grad_gain_two = jnp.sum(grad_second * normed_two, axis=0)
    grad_bias_two = jnp.sum(grad_second, axis=0)
    input_grad = (
        grad_float
        + norm_back(grad_first, normed_one, inverse_one, gain_one_b)
        + norm_back(grad_second, normed_two, inverse_two, gain_two_b)
    )
    local_grads = (
        grad_gain_one,
        grad_bias_one,
        grad_gain_two,
        grad_bias_two,
        grad_w_qkv,
        grad_b_qkv,
        grad_w_out,
        bias_total,
        grad_w_up,
        grad_b_up,
        grad_w_down,
        bias_total,
    )
    owned = (
        lax.psum_scatter(
            local_grads[0].astype(jnp.bfloat16), "fsdp", scatter_dimension=0, tiled=True
        ).astype(jnp.float32),
        lax.psum_scatter(
            local_grads[1].astype(jnp.bfloat16), "fsdp", scatter_dimension=0, tiled=True
        ).astype(jnp.float32),
        lax.psum_scatter(
            local_grads[2].astype(jnp.bfloat16), "fsdp", scatter_dimension=0, tiled=True
        ).astype(jnp.float32),
        lax.psum_scatter(
            local_grads[3].astype(jnp.bfloat16), "fsdp", scatter_dimension=0, tiled=True
        ).astype(jnp.float32),
        lax.psum_scatter(
            local_grads[4].astype(jnp.bfloat16), "fsdp", scatter_dimension=0, tiled=True
        ).astype(jnp.float32),
        lax.psum_scatter(
            local_grads[5].astype(jnp.bfloat16), "fsdp", scatter_dimension=0, tiled=True
        ).astype(jnp.float32),
        lax.psum_scatter(
            local_grads[6].astype(jnp.bfloat16), "fsdp", scatter_dimension=0, tiled=True
        ).astype(jnp.float32),
        lax.psum_scatter(
            local_grads[7].astype(jnp.bfloat16), "fsdp", scatter_dimension=0, tiled=True
        ).astype(jnp.float32),
        lax.psum_scatter(
            local_grads[8].astype(jnp.bfloat16), "fsdp", scatter_dimension=0, tiled=True
        ).astype(jnp.float32),
        lax.psum_scatter(
            local_grads[9].astype(jnp.bfloat16), "fsdp", scatter_dimension=0, tiled=True
        ).astype(jnp.float32),
        lax.psum_scatter(
            local_grads[10].astype(jnp.bfloat16), "fsdp", scatter_dimension=0, tiled=True
        ).astype(jnp.float32),
        lax.psum_scatter(
            local_grads[11].astype(jnp.bfloat16), "fsdp", scatter_dimension=0, tiled=True
        ).astype(jnp.float32),
    )
    summed = (
        lax.psum(owned[0].astype(jnp.bfloat16), "dp").astype(jnp.float32),
        lax.psum(owned[1].astype(jnp.bfloat16), "dp").astype(jnp.float32),
        lax.psum(owned[2].astype(jnp.bfloat16), "dp").astype(jnp.float32),
        lax.psum(owned[3].astype(jnp.bfloat16), "dp").astype(jnp.float32),
        lax.psum(owned[4].astype(jnp.bfloat16), "dp").astype(jnp.float32),
        lax.psum(owned[5].astype(jnp.bfloat16), "dp").astype(jnp.float32),
        lax.psum(owned[6].astype(jnp.bfloat16), "dp").astype(jnp.float32),
        lax.psum(owned[7].astype(jnp.bfloat16), "dp").astype(jnp.float32),
        lax.psum(owned[8].astype(jnp.bfloat16), "dp").astype(jnp.float32),
        lax.psum(owned[9].astype(jnp.bfloat16), "dp").astype(jnp.float32),
        lax.psum(owned[10].astype(jnp.bfloat16), "dp").astype(jnp.float32),
        lax.psum(owned[11].astype(jnp.bfloat16), "dp").astype(jnp.float32),
    )
    return (
        layer_output,
        input_grad[None],
        summed[0],
        summed[1],
        summed[2],
        summed[3],
        summed[4],
        summed[5],
        summed[6],
        summed[7],
        summed[8],
        summed[9],
        summed[10],
        summed[11],
    )


def solution(mesh):
    placed = (
        P("dp", "fsdp", None),
        P("fsdp"),
        P("fsdp"),
        P("fsdp"),
        P("fsdp"),
        P("fsdp", None),
        P("fsdp"),
        P("fsdp", None),
        P("fsdp"),
        P("fsdp", None),
        P("fsdp"),
        P("fsdp", None),
        P("fsdp"),
        P("dp", "fsdp", None),
    )
    return jax.shard_map(
        body,
        mesh=mesh,
        in_specs=placed,
        out_specs=(
            P("dp", "fsdp", None),
            P("dp", "fsdp", None),
            P("fsdp"),
            P("fsdp"),
            P("fsdp"),
            P("fsdp"),
            P("fsdp", None),
            P("fsdp"),
            P("fsdp", None),
            P("fsdp"),
            P("fsdp", None),
            P("fsdp"),
            P("fsdp", None),
            P("fsdp"),
        ),
        check_vma=False,
    )
```

profile of v0, /device:TPU:0, one launch (start us, length us, event | category | flops | bytes accessed | tf_op | source)
XLA Modules:
  0.0 913.9 jit_solution(2725459550871398994)
XLA Ops:
  8.7 1.3 fusion.76
  11.4 0.8 dynamic-update-slice
  12.2 0.8 dynamic-update-slice.1
  13.0 0.8 dynamic-update-slice.4
  13.9 0.8 dynamic-update-slice.5
  14.7 0.9 dynamic-update-slice.2
  15.6 40.5 %all-reduce.15 = (bf16[768]{0:T(1024)(128)(2,1)}, bf16[768]{0:T(1024)(128)(2,1)}, bf16[2304]{0:T(1024)(128)(2,1)S(1)}, bf16[768]{0:T(1024)(128)(2,1)S(1)}, bf16[768]{0:T(1024)(128)(2,1)S(1)}) all-reduce(bf16[768]{0:T(1024)(128)(2,1)S(1)} %dynamic-update-slice.5, ...), channel_id=1, replica_groups=mesh['dp'=4,'fsdp'=8] {'fsdp'}, use_global_device_ids=true, to_apply=%add.5 | all-reduce | flops 5376 | bytes 21504
  56.2 1.0 convert_reduce_fusion
  57.3 1.1 fusion.62
  59.1 18.8 %all-gather.8.cloned.1.call-done = bf16[768,2304]{1,0:T(8,128)(2,1)} async-done(((bf16[96,2304]{1,0:T(8,128)(2,1)}), bf16[768,2304]{1,0:T(8,128)(2,1)}) %all-gather.8.cloned.1.call-update) | async-done | bytes 3538960 | tf_op jit(solution)/shard_map/all_gather | solution.py:94
  77.9 2.8 convolution_add_fusion
  84.0 36.1 %all-gather.14.cloned.1.call-done = bf16[768,768]{1,0:T(8,128)(2,1)} async-done(((bf16[96,768]{1,0:T(8,128)(2,1)}), bf16[768,768]{1,0:T(8,128)(2,1)}) %all-gather.14.cloned.1.call-update) | async-done | bytes 1179664 | tf_op jit(solution)/shard_map/all_gather | solution.py:96
  120.1 1.8 convolution_convert_fusion.4
  122.1 43.7 %all-gather.12.cloned.1.call-done = bf16[1024,768]{0,1:T(8,128)(2,1)} async-done(((bf16[128,768]{0,1:T(8,128)(2,1)}), bf16[1024,768]{0,1:T(8,128)(2,1)}) %all-gather.12.cloned.1.call-update) | async-done | bytes 1572880 | tf_op jit(solution)/shard_map/all_gather | solution.py:142
  165.8 2.8 while.42
  165.8 1.2 constant_dynamic-slice_fusion.8
  168.6 42.2 %all-gather.10.cloned.1.call-done = bf16[1024,768]{1,0:T(8,128)(2,1)} async-done(((bf16[128,768]{1,0:T(8,128)(2,1)}), bf16[1024,768]{1,0:T(8,128)(2,1)}) %all-gather.10.cloned.1.call-update) | async-done | bytes 1572880 | tf_op jit(solution)/shard_map/all_gather | solution.py:143
  210.8 1.7 copy.60
  212.6 0.8 broadcast.241.clone
  213.4 5.3 while.43
  213.4 1.3 constant_dynamic-slice_fusion.9
  214.7 0.8 broadcast_compare_fusion.7
  215.4 3.2 fusion.134
  218.7 1.9 fusion.75
  220.6 1.3 broadcast_in_dim.113
  221.9 1.4 broadcast_in_dim.113.clone
  223.3 0.8 broadcast.241
  224.1 6.6 while.44
  225.1 1.2 fusion.146
  228.3 0.7 copy-done.2
  229.0 1.6 bitcast_dynamic-update-slice_fusion.5
  230.7 2.6 copy.67
  233.4 2.7 copy.69
  236.2 0.8 copy-done.8
  237.0 1.5 convolution_convert_fusion.3
  238.6 38.4 %all-gather = bf16[8,1,384]{2,1,0:T(2,128)(2,1)S(1)} all-gather(bf16[1,1,384]{2,1,0:T(2,128)(2,1)S(1)} %reshape.321), channel_id=1, replica_groups=mesh['dp'=4,'fsdp'=8] {'fsdp'}, dimensions={0}, use_global_device_ids=true | all-gather | bytes 6912 | tf_op jit(solution)/shard_map/all_gather | solution.py:99
  277.0 13.8 %all-gather.16.cloned.1.call-done = bf16[768,3072]{1,0:T(8,128)(2,1)} async-done(((bf16[96,3072]{1,0:T(8,128)(2,1)}), bf16[768,3072]{1,0:T(8,128)(2,1)}) %all-gather.16.cloned.1.call-update) | async-done | bytes 4718608 | tf_op jit(solution)/shard_map/all_gather | solution.py:98
  290.8 7.6 fusion.20
  298.4 72.2 %all-gather.18.cloned.1.call-done = bf16[3072,768]{1,0:T(8,128)(2,1)} async-done(((bf16[384,768]{1,0:T(8,128)(2,1)}), bf16[3072,768]{1,0:T(8,128)(2,1)}) %all-gather.18.cloned.1.call-update) | async-done | bytes 4718608 | tf_op jit(solution)/shard_map/all_gather | solution.py:100
  370.6 5.2 fusion.77
  375.8 3.8 convolution_convert_fusion.1
  379.6 3.5 convolution_convert_fusion
  383.2 0.9 copy-done.3
  384.9 53.3 %reduce-scatter.19.cloned.1.call-done = bf16[128,768]{1,0:T(8,128)(2,1)} async-done(((bf16[1024,768]{1,0:T(8,128)(2,1)}), bf16[128,768]{1,0:T(8,128)(2,1)}) %reduce-scatter.19.cloned.1.call-update) | async-done | bytes 196624
  438.1 1.1 copy.68
  439.9 66.0 %reduce-scatter.21.cloned.1.call-done = bf16[128,768]{1,0:T(8,128)(2,1)} async-done(((bf16[1024,768]{1,0:T(8,128)(2,1)}), bf16[128,768]{1,0:T(8,128)(2,1)}) %reduce-scatter.21.cloned.1.call-update) | async-done | bytes 196624
  505.9 1.1 copy.70
  507.7 1.0 pad_maximum_fusion.2
  508.8 3.7 convolution_convert_fusion.2
  515.3 4.2 fusion.79
  519.8 1.5 fusion.60
  521.3 35.0 %all-reduce.14 = (bf16[768]{0:T(1024)(128)(2,1)S(1)}, bf16[768]{0:T(1024)(128)(2,1)S(1)}, bf16[768]{0:T(1024)(128)(2,1)S(1)}, bf16[768]{0:T(1024)(128)(2,1)S(1)}...) all-reduce(bf16[768]{0:T(1024)(128)(2,1)S(1)} %dynamic-update-slice, ...), channel_id=1, replica_groups=mesh['dp'=4,'fsdp'=8] {'fsdp'}, use_global_device_ids=true, to_apply=%add.6 | all-reduce | flops 10752 | bytes 43008
  556.8 5.7 all-reduce.16
  565.8 3.1 convolution_add_fusion.3
  568.9 4.7 reduce-scatter.13.cloned.1.call-done
  573.7 98.1 %reduce-scatter.15.cloned.1.call-done = bf16[96,3072]{1,0:T(8,128)(2,1)} async-done(((bf16[768,3072]{1,0:T(8,128)(2,1)}), bf16[96,3072]{1,0:T(8,128)(2,1)}) %reduce-scatter.15.cloned.1.call-update) | async-done | bytes 589840 | tf_op jit(solution)/shard_map/reduce_scatter | solution.py:328
  671.8 99.0 %reduce-scatter.17.cloned.1.call-done = bf16[384,768]{1,0:T(8,128)(2,1)} async-done(((bf16[3072,768]{1,0:T(8,128)(2,1)}), bf16[384,768]{1,0:T(8,128)(2,1)}) %reduce-scatter.17.cloned.1.call-update) | async-done | bytes 589840 | tf_op jit(solution)/shard_map/reduce_scatter | solution.py:334
  770.8 82.6 %reduce-scatter.11.cloned.1.call-done = bf16[96,2304]{1,0:T(8,128)(2,1)} async-done(((bf16[768,2304]{1,0:T(8,128)(2,1)}), bf16[96,2304]{1,0:T(8,128)(2,1)}) %reduce-scatter.11.cloned.1.call-update) | async-done | bytes 442384 | tf_op jit(solution)/shard_map/reduce_scatter | solution.py:316
  853.5 1.0 fusion.35
  854.5 1.0 fusion.56
  855.5 46.3 %all-reduce.20.cloned.1.call-done = (bf16[96,2304]{1,0:T(8,128)(2,1)}, bf16[96,768]{1,0:T(8,128)(2,1)}, bf16[96,3072]{1,0:T(8,128)(2,1)}, bf16[384,768]{1,0:T(8,128)(2,1)}) async-done(((bf16[96,2304]{1,0:T(8,128)(2,1)}, bf16[96,768]{1,0:T(8,128)(2,1)}, bf16[96,3072]{1,0:T(8,128)(2,1)}, bf16[384,768]{1,0:T(8,128)(2,1)}), (bf16[96,2304]{1,0:T(8,128)(2,1)}, bf16[96,768]{1,0:T(8,128)(2,1)}, ...) | async-done | bytes 1769488 | tf_op jit(solution)/shard_map/psum | solution.py:346
  901.8 2.3 convert_element_type.239
  904.1 1.1 convert_element_type.242
  905.1 1.0 convert_element_type.233
  (171 shorter events, 18.8 us)
Async XLA Ops:
  7.2 70.8 %all-gather.8.cloned.1.call-start = ((), (), s32[]{:S(2)}) async-start(), calls=%async_computation.6 | async-start | bytes 3981312 | tf_op jit(solution)/shard_map/all_gather | solution.py:94
  7.9 112.2 %all-gather.14.cloned.1.call-start = ((), (), s32[]{:S(2)}) async-start(), calls=%async_computation.9 | async-start | bytes 1327104 | tf_op jit(solution)/shard_map/all_gather | solution.py:96
  8.7 157.2 %all-gather.12.cloned.1.call-start = ((), (), s32[]{:S(2)}) async-start(), calls=%async_computation.8 | async-start | bytes 1769472 | tf_op jit(solution)/shard_map/all_gather | solution.py:142
  56.1 24.6 %copy-start.14 = (f32[768]{0:T(1024)}, f32[768]{0:T(1024)S(1)}, u32[]{:S(2)}) copy-start(f32[768]{0:T(1024)S(1)} %convert_element_type.199) | copy-start | bytes 9220
  56.1 24.6 %copy-start.16 = (f32[768]{0:T(1024)}, f32[768]{0:T(1024)S(1)}, u32[]{:S(2)}) copy-start(f32[768]{0:T(1024)S(1)} %convert_element_type.200) | copy-start | bytes 9220
  57.2 23.5 %copy-start.21 = (f32[128]{0:T(128)}, f32[128]{0:T(128)S(1)}, u32[]{:S(2)}) copy-start(f32[128]{0:T(128)S(1)} %broadcast_multiply_fusion.6) | copy-start | bytes 1540
  58.4 22.4 %copy-start.24 = (f32[128]{0:T(128)}, f32[128]{0:T(128)S(1)}, u32[]{:S(2)}) copy-start(f32[128]{0:T(128)S(1)} %add_rsqrt_fusion) | copy-start | bytes 1540
  59.1 22.1 %copy-start.19 = (f32[128,8]{0,1:T(8,128)}, f32[128,8]{0,1:T(8,128)S(1)}, u32[]{:S(2)}) copy-start(f32[128,8]{0,1:T(8,128)S(1)} %get-tuple-element.522) | copy-start | bytes 12292
  81.2 38.9 %copy-start.7 = (bf16[1,128,768]{2,1,0:T(8,128)(2,1)S(1)}, bf16[1,128,768]{2,1,0:T(8,128)(2,1)}, u32[]{:S(2)}) copy-start(bf16[1,128,768]{2,1,0:T(8,128)(2,1)} %param.33) | copy-start | bytes 589828
  82.0 128.8 %all-gather.10.cloned.1.call-start = ((), (), s32[]{:S(2)}) async-start(), calls=%async_computation.7 | async-start | bytes 1769472 | tf_op jit(solution)/shard_map/all_gather | solution.py:143
  82.8 208.0 %all-gather.16.cloned.1.call-start = ((), (), s32[]{:S(2)}) async-start(), calls=%async_computation.10 | async-start | bytes 5308416 | tf_op jit(solution)/shard_map/all_gather | solution.py:98
  83.4 287.2 %all-gather.18.cloned.1.call-start = ((), (), s32[]{:S(2)}) async-start(), calls=%async_computation.11 | async-start | bytes 5308416 | tf_op jit(solution)/shard_map/all_gather | solution.py:100
  83.9 354.2 %reduce-scatter.19.cloned.1.call-start = ((), (), s32[]{:S(2)}) async-start(), calls=%async_computation.16 | async-start | bytes 1769472
  168.6 44.7 %copy-start = (bf16[1024,768]{0,1:T(8,128)(2,1)S(1)}, bf16[1024,768]{0,1:T(8,128)(2,1)}, u32[]{:S(2)}) copy-start(bf16[1024,768]{0,1:T(8,128)(2,1)} %get-tuple-element.878) | copy-start | bytes 4718596
  225.1 1.4 copy-start.5
  226.5 1.0 copy-start.1
  227.2 1.1 copy-start.6
  228.3 0.7 copy-start.2
  233.3 272.6 %reduce-scatter.21.cloned.1.call-start = ((), (), s32[]{:S(2)}) async-start(), calls=%async_computation.17 | async-start | bytes 1769472
  236.0 0.9 copy-start.8
  236.0 1.0 copy-start.11
  236.0 2.5 copy-start.29
  236.1 2.5 copy-start.28
  236.1 2.6 copy-start.30
  236.1 54.7 %copy-start.4 = (bf16[1,128,768]{2,1,0:T(8,128)(2,1)S(1)}, bf16[1,128,768]{2,1,0:T(8,128)(2,1)}, u32[]{:S(2)}) copy-start(bf16[1,128,768]{2,1,0:T(8,128)(2,1)} %param.20) | copy-start | bytes 589828
  236.1 54.7 %copy-start.22 = (f32[128]{0:T(128)S(1)}, f32[128]{0:T(128)}, u32[]{:S(2)}) copy-start(f32[128]{0:T(128)} %copy-done.21) | copy-start | bytes 1540
  236.1 54.7 %copy-start.25 = (f32[128]{0:T(128)S(1)}, f32[128]{0:T(128)}, u32[]{:S(2)}) copy-start(f32[128]{0:T(128)} %copy-done.24) | copy-start | bytes 1540
  236.1 337.6 %reduce-scatter.13.cloned.1.call-start = ((), (), s32[]{:S(2)}) async-start(), calls=%async_computation.13 | async-start | bytes 1327104 | tf_op jit(solution)/shard_map/reduce_scatter | solution.py:322
  238.5 433.3 %reduce-scatter.15.cloned.1.call-start = ((), (), s32[]{:S(2)}) async-start(), calls=%async_computation.14 | async-start | bytes 5308416 | tf_op jit(solution)/shard_map/reduce_scatter | solution.py:328
  379.5 391.3 %reduce-scatter.17.cloned.1.call-start = ((), (), s32[]{:S(2)}) async-start(), calls=%async_computation.15 | async-start | bytes 5308416 | tf_op jit(solution)/shard_map/reduce_scatter | solution.py:334
  383.1 1.0 copy-start.3
  383.2 123.9 %copy-start.20 = (f32[128,8]{0,1:T(8,128)S(1)}, f32[128,8]{0,1:T(8,128)}, u32[]{:S(2)}) copy-start(f32[128,8]{0,1:T(8,128)} %copy-done.19) | copy-start | bytes 12292
  383.2 470.3 %reduce-scatter.11.cloned.1.call-start = ((), (), s32[]{:S(2)}) async-start(), calls=%async_computation.12 | async-start | bytes 3981312 | tf_op jit(solution)/shard_map/reduce_scatter | solution.py:316
  384.2 124.6 %copy-start.15 = (f32[768]{0:T(1024)S(1)}, f32[768]{0:T(1024)}, u32[]{:S(2)}) copy-start(f32[768]{0:T(1024)} %copy-done.14) | copy-start | bytes 9220
  384.2 124.6 %copy-start.17 = (f32[768]{0:T(1024)S(1)}, f32[768]{0:T(1024)}, u32[]{:S(2)}) copy-start(f32[768]{0:T(1024)} %copy-done.16) | copy-start | bytes 9220
  512.5 2.3 copy-start.31
  512.5 2.6 copy-start.32
  512.5 389.2 %all-reduce.20.cloned.1.call-start = ((), (), s32[]{:S(2)}) async-start(), calls=%async_computation.18 | async-start | bytes 3538944 | tf_op jit(solution)/shard_map/psum | solution.py:346
  515.3 4.5 copy-start.10
  515.3 4.5 copy-start.23
  515.3 4.5 copy-start.26
  519.8 1.5 copy-start.27
  563.7 343.1 %copy-start.33 = (f32[96]{0:T(128)}, f32[96]{0:T(128)S(1)}, u32[]{:S(2)}) copy-start(f32[96]{0:T(128)S(1)} %convert_element_type.237) | copy-start | bytes 1156
  568.9 284.5 %copy-start.9 = (bf16[768,768]{1,0:T(8,128)(2,1)S(1)}, bf16[768,768]{1,0:T(8,128)(2,1)}, u32[]{:S(2)}) copy-start(bf16[768,768]{1,0:T(8,128)(2,1)} %all-gather.14.cloned.1.call-done) | copy-start | bytes 3538948
  901.8 2.3 copy-start.12
  901.8 3.4 copy-start.13
  904.0 2.1 copy-start.18
Sparse Core Ops, SparseCore 0:
  10.2 67.7 all-gather.7
  80.1 39.9 all-gather.13
  122.7 43.0 all-gather.11
  168.5 42.3 all-gather.9
  212.9 77.8 all-gather.15
  292.8 77.7 all-gather.17
  374.0 64.0 reduce-scatter.18
  441.5 64.3 reduce-scatter.20
  509.9 63.7 reduce-scatter.12
  577.2 94.5 reduce-scatter.14
  675.4 95.3 reduce-scatter.16
  774.3 79.0 reduce-scatter.10
  856.0 45.7 all-reduce.19
where the time goes:
time: 915 us; the launch traced here: 914 us
  waiting for transfers between devices  679 us (74%)
  blocking collectives  120 us (13%)
  matrix products  48.3 us (5%)
  local copies, waits for them, and re-layouts  29.3 us (3%)
  other arithmetic  18.8 us (2%)
  between operations  17.7 us (2%)
    unnamed x15, waiting for transfers between devices  122 us
    reduce_scatter x1, waiting for transfers between devices, body(): lax.psum_scatter(local_grads[10].astype(jnp.bfloat16), 'fsdp', scatter_di...  99 us
    reduce_scatter x1, waiting for transfers between devices, body(): lax.psum_scatter(local_grads[8].astype(jnp.bfloat16), 'fsdp', scatter_dim...  98.1 us
    reduce_scatter x1, waiting for transfers between devices, body(): lax.psum_scatter(local_grads[4].astype(jnp.bfloat16), 'fsdp', scatter_dim...  82.6 us
    unnamed x2, blocking collectives  75.5 us
    all_gather x1, waiting for transfers between devices, body(): lax.all_gather(down_weight, 'fsdp', axis=0, tiled=True)  72.2 us
    psum x1, waiting for transfers between devices, body(): lax.psum(owned[4].astype(jnp.bfloat16), 'dp').astype(jnp.float32)  46.3 us
    all_gather x1, waiting for transfers between devices, body(): lax.all_gather(key_local, 'fsdp', axis=0, tiled=True)  43.7 us
  transfers between devices with their start and end apart: 13, of which 13 were waited for; matrix products, arithmetic and copies ran while one was open for 10% of the time, Pallas kernels for 0%

commit v1 on v0

v1 whole, which is shorter than its diff:
```python
import math

import jax
import jax.numpy as jnp
from jax import lax
from jax.sharding import PartitionSpec as P

HEADS = 12
HEAD = 64
ROT = 16

epsilon = 1e-05
inv_root_two = 1.0 / math.sqrt(2.0)
inv_root_twopi = 1.0 / math.sqrt(2.0 * math.pi)
bf16 = jnp.bfloat16
f32 = jnp.float32


def rotary(tensor, cosine, sine, direction):
    half = ROT // 2
    first = tensor[..., :half]
    second = tensor[..., half:ROT]
    return jnp.concatenate(
        [
            first * cosine - direction * second * sine,
            second * cosine + direction * first * sine,
            tensor[..., ROT:],
        ],
        axis=-1,
    )


def dot(a, b, dims):
    return lax.dot_general(a, b, ((dims[0], dims[1]), ((), ())), preferred_element_type=f32)


NN = ((1,), (0,))
NT = ((1,), (1,))
TN = ((0,), (0,))


def gather_rows(arrays):
    return [lax.all_gather(a, "fsdp", axis=0, tiled=True) for a in arrays]


def scatter_rows(a):
    return lax.psum_scatter(a, "fsdp", scatter_dimension=0, tiled=True)


def spread_weights(blocks):
    return lax.all_to_all(blocks, "fsdp", 0, 0, tiled=True)


def return_grads(blocks, own):
    summed = lax.psum(blocks, "dp")
    own = lax.psum(own, "dp")
    return lax.all_to_all(summed, "fsdp", 0, 0, tiled=True), own


def body(
    tokens,
    ln1_gain,
    ln1_bias,
    ln2_gain,
    ln2_bias,
    qkv_weight,
    qkv_bias,
    out_weight,
    out_bias,
    up_weight,
    up_bias,
    down_weight,
    down_bias,
    cotangent,
):
    rank = lax.axis_index("fsdp")
    F = lax.axis_size("fsdp")
    rows, D = tokens.shape[1:]
    W = D // F
    FFW = down_weight.shape[0]
    NH = max(-(-((g * W) % HEAD + W) // HEAD) for g in range(F))
    WIN = NH * HEAD
    starts = [min(g * W // HEAD, HEADS - NH) * HEAD for g in range(F)]
    start = jnp.minimum(rank * W // HEAD, HEADS - NH) * HEAD
    off = rank * W - start
    S = rows * F

    qkv3 = qkv_weight.reshape(W, 3, D)
    blocks = jnp.stack(
        [
            jnp.concatenate(
                [
                    qkv3[:, 0, s : s + WIN],
                    qkv3[:, 1, s : s + WIN],
                    qkv3[:, 2, s : s + WIN],
                    up_weight[:, g * FFW : (g + 1) * FFW],
                ],
                axis=1,
            )
            for g, s in enumerate(starts)
        ]
    )
    smalls = jnp.concatenate(
        [ln1_gain, ln1_bias, ln2_gain, ln2_bias, out_bias, down_bias, qkv_bias]
    )[None]
    x_low, small_all = gather_rows([tokens[0], smalls])
    wall = spread_weights(blocks).reshape(D, 3 * WIN + FFW)
    w_qkv = wall[:, : 3 * WIN]
    w_up = wall[:, 3 * WIN :]
    up_ring = [(i, (i + 1) % F) for i in range(F)]
    down_ring = [(i, (i - 1) % F) for i in range(F)]
    out_prev = lax.ppermute(out_weight, "fsdp", up_ring)
    out_next = lax.ppermute(out_weight, "fsdp", down_ring)
    (grad_out,) = gather_rows([cotangent[0]])
    out_three = jnp.concatenate(
        [out_prev, out_weight, out_next, jnp.zeros((WIN, D), bf16)], axis=0
    )
    w_out_win = lax.dynamic_slice_in_dim(out_three, W - off, WIN, 0)
    win_col = jnp.arange(WIN, dtype=jnp.int32)
    mine = (win_col >= off) & (win_col < off + W)
    small_all = small_all.astype(f32)
    gain_one, bias_one, gain_two, bias_two, b_out, b_down = [
        small_all[:, i * W : (i + 1) * W].reshape(D) for i in range(6)
    ]
    b_qkv = small_all[:, 6 * W :].reshape(3, D)
    b_qkv = lax.dynamic_slice_in_dim(b_qkv, start, WIN, 1).reshape(3 * WIN)
    b_up = up_bias.astype(f32)

    x = x_low.astype(f32)
    center = x - jnp.mean(x, axis=-1, keepdims=True)
    inverse = lax.rsqrt(jnp.mean(center * center, axis=-1, keepdims=True) + epsilon)
    normed = center * inverse
    first_low = (normed * gain_one + bias_one).astype(bf16)
    second_low = (normed * gain_two + bias_two).astype(bf16)

    places = jnp.arange(S, dtype=f32)
    half = ROT // 2
    freq = 10000.0 ** (-(jnp.arange(half, dtype=f32) * 2.0) / ROT)
    angle = places[:, None] * freq[None, :]
    cosine = jnp.cos(angle)[:, None, :]
    sine = jnp.sin(angle)[:, None, :]

    proj = dot(first_low, w_qkv, NN) + b_qkv
    queries = (rotary(proj[:, :WIN].reshape(S, NH, HEAD), cosine, sine, 1.0) * 0.125).astype(bf16)
    keys = rotary(proj[:, WIN : 2 * WIN].reshape(S, NH, HEAD), cosine, sine, 1.0).astype(bf16)
    vals = proj[:, 2 * WIN :].astype(bf16).reshape(S, NH, HEAD)
    q_place = jnp.arange(S, dtype=jnp.int32)
    visible = (q_place[None, :] <= q_place[:, None])[None]
    scores = jnp.einsum("qhd,khd->hqk", queries, keys, preferred_element_type=f32)
    masked = jnp.where(visible, scores, -1e30)
    top = jnp.max(masked, axis=-1, keepdims=True)
    lse = top + jnp.log(jnp.sum(jnp.exp(masked - top), axis=-1, keepdims=True))
    probs = jnp.exp(masked - lse)
    probs_low = probs.astype(bf16)
    attended = jnp.einsum("hqk,khd->qhd", probs_low, vals, preferred_element_type=f32)
    att_low = jnp.where(mine, attended.reshape(S, WIN), 0.0).astype(bf16)

    hidden_pre = dot(second_low, w_up, NN) + b_up
    cdf = 0.5 * (1.0 + lax.erf(hidden_pre * inv_root_two))
    hidden_low = (hidden_pre * cdf).astype(bf16)
    part = dot(att_low, w_out_win, NN) + dot(hidden_low, down_weight, NN)
    branch = scatter_rows(part.astype(bf16)).astype(f32)

    grad_hidden = dot(grad_out, down_weight, NT)
    slope = cdf + hidden_pre * jnp.exp(-0.5 * hidden_pre * hidden_pre) * inv_root_twopi
    grad_pre = (grad_hidden * slope).astype(bf16)
    grad_w_down = dot(hidden_low, grad_out, TN)
    grad_w_out_win = dot(att_low, grad_out, TN)
    grad_w_out = lax.dynamic_slice_in_dim(grad_w_out_win, off, W, 0)
    bias_total = jnp.sum(grad_out.astype(f32), axis=0)
    grad_b_up = jnp.sum(grad_pre.astype(f32), axis=0)
    grad_att = dot(grad_out, w_out_win, NT).astype(bf16).reshape(S, NH, HEAD)
    delta = jnp.transpose(jnp.sum(grad_att.astype(f32) * attended, axis=-1))[:, :, None]
    grad_probs = jnp.einsum("qhd,khd->hqk", grad_att, vals, preferred_element_type=f32)
    grad_scores = (probs * (grad_probs - delta)).astype(bf16)
    grad_q = jnp.einsum("hqk,khd->qhd", grad_scores, keys, preferred_element_type=f32)
    grad_k = jnp.einsum("hqk,qhd->khd", grad_scores, queries, preferred_element_type=f32)
    grad_v = jnp.einsum("hqk,qhd->khd", probs_low, grad_att, preferred_element_type=f32)
    grad_proj = jnp.stack(
        [
            rotary(grad_q * 0.125, cosine, sine, -1.0).reshape(S, WIN),
            rotary(grad_k, cosine, sine, -1.0).reshape(S, WIN),
            grad_v.reshape(S, WIN),
        ],
        axis=1,
    )
    grad_proj = jnp.where(mine, grad_proj, 0.0).astype(bf16).reshape(S, 3 * WIN)
    grad_w_qkv = dot(first_low, grad_proj, TN)
    grad_w_up = dot(second_low, grad_pre, TN)
    grad_b_qkv = jnp.sum(grad_proj.astype(f32), axis=0).reshape(3, WIN)
    grad_first = dot(grad_proj, w_qkv, NT)
    grad_second = dot(grad_pre, w_up, NT)
    vectors = [
        jnp.sum(grad_first * normed, axis=0),
        jnp.sum(grad_first, axis=0),
        jnp.sum(grad_second * normed, axis=0),
        jnp.sum(grad_second, axis=0),
    ]
    mixed = grad_first * gain_one + grad_second * gain_two
    b_full = lax.dynamic_update_slice_in_dim(jnp.zeros((3, D), f32), grad_b_qkv, start, 1)
    small_part = jnp.concatenate(
        [v.reshape(F, W) for v in vectors] + [b_full.reshape(F, 3 * W)], axis=1
    )
    mixed_mine = scatter_rows(mixed.astype(bf16)).astype(f32)
    small_mine = scatter_rows(small_part)[0]
    own_small = jnp.concatenate(
        [small_mine, lax.dynamic_slice_in_dim(bias_total, rank * W, W, 0), grad_b_up]
    )
    own_small = lax.psum(own_small, "dp")

    grad_blocks = jnp.concatenate([grad_w_qkv, grad_w_up], axis=1).astype(bf16)
    grad_blocks = grad_blocks.reshape(F, W, 3 * WIN + FFW)
    own = jnp.concatenate([grad_w_out, grad_w_down], axis=0).astype(bf16)
    returned, own = return_grads(grad_blocks, own)
    returned = returned.astype(f32)
    own = own.astype(f32)
    pieces = [
        [returned[g, :, i * WIN + g * W - s : i * WIN + g * W - s + W] for g, s in enumerate(starts)]
        for i in range(3)
    ]
    out_w_qkv = jnp.concatenate(pieces[0] + pieces[1] + pieces[2], axis=1)
    out_w_up = jnp.concatenate([returned[g, :, 3 * WIN :] for g in range(F)], axis=1)

    here = rank * rows
    x_own = tokens[0].astype(f32)
    c_own = x_own - jnp.mean(x_own, axis=-1, keepdims=True)
    i_own = lax.rsqrt(jnp.mean(c_own * c_own, axis=-1, keepdims=True) + epsilon)
    n_own = c_own * i_own
    layer_output = (x_own + branch + b_out + b_down).astype(bf16)
    input_grad = cotangent[0].astype(f32) + i_own * (
        mixed_mine
        - jnp.mean(mixed_mine, axis=-1, keepdims=True)
        - n_own * jnp.mean(mixed_mine * n_own, axis=-1, keepdims=True)
    )
    g = [own_small[i * W : (i + 1) * W] for i in range(4)]
    bias_mine = own_small[7 * W : 8 * W]
    return (
        layer_output[None],
        input_grad[None],
        g[0],
        g[1],
        g[2],
        g[3],
        out_w_qkv,
        own_small[4 * W : 7 * W],
        own[:W],
        bias_mine,
        out_w_up,
        own_small[8 * W :],
        own[W:],
        bias_mine,
    )


def solution(mesh):
    row = P("fsdp", None)
    vec = P("fsdp")
    act = P("dp", "fsdp", None)
    return jax.shard_map(
        body,
        mesh=mesh,
        in_specs=(act, vec, vec, vec, vec, row, vec, row, vec, row, vec, row, vec, act),
        out_specs=(act, act, vec, vec, vec, vec, row, vec, row, vec, row, vec, row, vec),
        check_vma=False,
    )
```

time: 915 us -> 363 us (0.40)
  waiting for transfers between devices: 679 us -> 106 us
  starting transfers between devices: 0.75 us -> 16.1 us
  blocking collectives: 120 us -> 134 us
    reduce_scatter x4 -> x2, waiting for transfers between devices: 284 us -> 51.2 us  [scatter_rows(): return lax.psum_scatter(a, 'fsdp', scatter_dimension=0, tiled=True)]
    all_gather x6 -> x2, waiting for transfers between devices: 227 us -> 6.78 us  [gather_rows(): return [lax.all_gather(a, 'fsdp', axis=0, tiled=True) for a in arrays]]
    unnamed x15 -> x5, waiting for transfers between devices: 122 us -> 1.27 us
    unnamed x2, blocking collectives: 75.5 us -> 128 us
    all_gather x1 -> x0, blocking collectives: 38.4 us -> none  [body(): lax.all_gather(up_bias, 'fsdp', axis=0, tiled=True)]
    all_to_all x0 -> x2, starting transfers between devices: none -> 9.77 us  [the longest x1 5.52 us: return_grads(): return (lax.all_to_all(summed, 'fsdp', 0, 0, tiled=True), own)]
    dot_general x19 -> x18, matrix products: 48.3 us -> 39.7 us  [the longest x12 23.6 us: dot(): lax.dot_general(a, b, ((dims[0], dims[1]), ((), ())), preferred_element_t...]
  transfers between devices with their start and end apart: 13 -> 9, of which waited for: 13 -> 3; matrix products, arithmetic and copies ran while one was open for 10% -> 12% of each run, Pallas kernels for 0% -> 0%
where the time goes in v1:
time: 363 us; the launch traced here: 362 us
  blocking collectives  134 us (37%)
  waiting for transfers between devices  106 us (29%)
  matrix products  39.7 us (11%)
  local copies, waits for them, and re-layouts  28.3 us (8%)
  other arithmetic  22.5 us (6%)
  starting transfers between devices  16.1 us (4%)
  between operations  15.3 us (4%)
    unnamed x2, blocking collectives  128 us
    reduce_scatter x2, waiting for transfers between devices, scatter_rows(): return lax.psum_scatter(a, 'fsdp', scatter_dimension=0, tiled=True)  51.2 us
    psum x1, waiting for transfers between devices, return_grads(): summed = lax.psum(blocks, 'dp')  46.5 us
    dot_general x12, matrix products, dot(): lax.dot_general(a, b, ((dims[0], dims[1]), ((), ())), preferred_element_t...  23.6 us
    unnamed x110, local copies, waits for them, and re-layouts  10.9 us
  transfers between devices with their start and end apart: 9, of which 3 were waited for; matrix products, arithmetic and copies ran while one was open for 12% of the time, Pallas kernels for 0%

profile of v1, /device:TPU:0, one launch (start us, length us, event | category | flops | bytes accessed | tf_op | source)
XLA Modules:
  0.0 361.6 jit_solution(6648687961368923165)
XLA Ops:
  7.2 3.0 collective-permute-start
  10.3 3.1 collective-permute-start.1
  13.4 1.6 reshape.208
  15.3 1.1 fusion.102
  16.6 0.7 fusion.74
  17.3 0.7 fusion.75
  18.0 0.7 fusion.76
  18.7 0.7 fusion.77
  19.4 0.7 fusion.78
  20.1 0.7 fusion.79
  20.8 0.7 fusion.80
  21.6 0.7 fusion.81
  22.3 4.2 %all-to-all-start = ((bf16[8,96,768]{2,1,0:T(8,128)(2,1)}), bf16[8,96,768]{2,1,0:T(8,128)(2,1)}, u32[]{:S(2)}, u32[]{:S(2)}) async-start(bf16[8,96,768]{2,1,0:T(8,128)(2,1)} %fusion.81), calls=%async_computation | async-start | bytes 2359296 | tf_op jit(solution)/shard_map/all_to_all | solution.py:51
  26.6 0.7 all-gather.8.cloned.1.call-update
  29.0 64.6 %all-reduce = bf16[6912]{0:T(1024)(128)(2,1)S(1)} all-reduce(bf16[6912]{0:T(1024)(128)(2,1)S(1)} %dynamic-update-slice), channel_id=3, replica_groups=mesh['dp'=4,'fsdp'=8] {'fsdp'}, use_global_device_ids=true, to_apply=%add | all-reduce | flops 6912 | bytes 27648
  93.9 0.7 fusion.105
  97.0 0.8 broadcast_multiply_fusion
  97.8 1.8 convert_reduce_fusion
  100.4 2.2 convolution_add_fusion.1
  102.7 0.7 slice.553
  104.2 1.7 select_reduce_fusion
  105.9 1.7 exponential_reduce_fusion
  107.7 1.5 copy-done.4
  109.8 6.8 %all-gather.8.cloned.1.call-done = bf16[1,1024,768]{2,1,0:T(8,128)(2,1)} async-done(((bf16[1,128,768]{2,1,0:T(8,128)(2,1)}), bf16[1,1024,768]{2,1,0:T(8,128)(2,1)}) %all-gather.8.cloned.1.call-update) | async-done | bytes 1572880 | tf_op jit(solution)/shard_map/all_gather | solution.py:43
  116.6 2.2 fusion.36
  118.9 6.5 %fusion.41 = (f32[1024,2]{0,1:T(2,128)S(1)}, bf16[2,64,1024]{2,1,0:T(8,128)(2,1)}) fusion(bf16[128,1024]{1,0:T(8,128)(2,1)S(1)} %fusion.36, bf16[1024,2,64]{0,2,1:T(8,128)(2,1)S(1)} %bitcast.330, f32[2,1024,1024]{1,2,0:T(8,128)} %copy-done.4, f32[2,1024]{1,0:T(2,128)S(1)} %copy-done.23, pred[1024,1024]{0,1:T(8,128)(4,1)S(1)} %iota_compare_fusion), kind=kOutput, calls=%fused_computation.73 | convolution fusion | flops 275249152 | bytes 10240000 | tf_op jit(solution)/shard_map/hqk,khd->qhd/dot_general | solution.py:155
  125.3 3.3 multiply_convert_fusion
  128.6 0.9 fusion.35
  129.6 1.4 convolution_bitcast_fusion
  131.0 2.4 fusion.83
  134.1 1.1 convert_reduce_fusion.3
  136.0 2.3 multiply_convert_fusion.1
  138.3 1.4 convert_reduce_fusion.2
  139.6 2.1 fusion.42
  141.7 1.8 convolution_convert_fusion
  144.2 4.6 %fusion.99 = (f32[768]{0:T(1024)S(1)}, f32[768]{0:T(1024)S(1)}, bf16[1024,768]{1,0:T(8,128)(2,1)}, f32[768]{0:T(1024)S(1)}, f32[768]{0:T(1024)S(1)}, /*index=5*/bf16[768,1024]{0,1:T(8,128)(2,1)}) fusion(f32[1024,768]{1,0:T(8,128)S(1)} %fusion.42, f32[1024]{0:T(1024)S(1)} %add_rsqrt_fusion, f32[1024]{0:T(1024)S(1)} %broadcast_multiply_fusion.1, ...), kind=kOutput, calls=%fused_computation.216 | convolution fusion | flops 616559616 | bytes 9270272 | tf_op jit(solution)/shard_map/dot_general | solution.py:34
  148.9 1.7 copy.54
  150.6 1.1 fusion.40
  151.7 2.2 convolution_convert_fusion.1
  153.9 1.1 pad_maximum_fusion.1
  155.0 0.7 copy-done.3
  156.1 0.8 fusion.32
  156.9 0.9 pad_maximum_fusion.2
  158.5 46.5 %all-reduce.5.cloned.1.call-done = (bf16[8,96,768]{2,1,0:T(8,128)(2,1)}, bf16[480,768]{1,0:T(8,128)(2,1)}) async-done(((bf16[8,96,768]{2,1,0:T(8,128)(2,1)}, bf16[480,768]{1,0:T(8,128)(2,1)}), (bf16[8,96,768]{2,1,0:T(8,128)(2,1)}, bf16[480,768]{1,0:T(8,128)(2,1)})) %all-reduce.5.cloned.1.call-update) | async-done | bytes 1916944 | tf_op jit(solution)/shard_map/psum | solution.py:55
  205.0 5.5 %all-to-all-start.1 = ((bf16[8,96,768]{2,1,0:T(8,128)(2,1)}), bf16[8,96,768]{2,1,0:T(8,128)(2,1)}, u32[]{:S(2)}, u32[]{:S(2)}) async-start(bf16[8,96,768]{2,1,0:T(8,128)(2,1)} %get-tuple-element.20), calls=%async_computation.3 | async-start | bytes 2359296 | tf_op jit(solution)/shard_map/all_to_all | solution.py:57
  212.1 63.2 %all-reduce.1 = f32[8,672]{1,0:T(8,128)S(1)} all-reduce(f32[8,672]{1,0:T(8,128)S(1)} %concatenate.80), channel_id=7, replica_groups=mesh['dp'=4,'fsdp'=8] {'fsdp'}, use_global_device_ids=true, to_apply=%region_16.17.clone | all-reduce | flops 5376 | bytes 43008
  276.0 6.1 %psum.21 = f32[1152]{0:T(1024)S(1)} all-reduce(f32[1152]{0:T(1024)S(1)} %concatenate.81), channel_id=1, replica_groups=mesh['dp'=4,'fsdp'=8] {'dp'}, use_global_device_ids=true, to_apply=%region_19.20 | all-reduce | flops 1152 | bytes 9216 | tf_op jit(solution)/shard_map/psum | solution.py:209
  283.3 1.0 fusion.110
  284.3 2.7 add_convert_fusion.1
  288.1 1.1 slice.478
  289.2 0.7 slice.467
  289.9 1.5 convert_element_type.125
  291.5 1.0 slice_bitcast_fusion.8
  292.5 2.3 concatenate.84
  294.9 0.7 fusion.73
  295.5 0.7 fusion.72
  296.2 0.7 fusion.71
  296.9 0.7 fusion.70
  297.6 0.7 fusion.69
  298.2 0.7 fusion.68
  298.9 0.7 fusion.67
  300.2 1.1 convert_reduce_fusion.4
  301.4 51.2 %reduce-scatter.3.cloned.1.call-done = bf16[128,768]{1,0:T(8,128)(2,1)} async-done(((bf16[1024,768]{1,0:T(8,128)(2,1)}), bf16[128,768]{1,0:T(8,128)(2,1)}) %reduce-scatter.3.cloned.1.call-update) | async-done | bytes 196624 | tf_op jit(solution)/shard_map/reduce_scatter | solution.py:47
  352.6 2.0 fusion.56
  (177 shorter events, 15.3 us)
Async XLA Ops:
  7.2 131.1 %copy-start = (bf16[384,768]{1,0:T(8,128)(2,1)S(1)}, bf16[384,768]{1,0:T(8,128)(2,1)}, u32[]{:S(2)}) copy-start(bf16[384,768]{1,0:T(8,128)(2,1)} %param.25) | copy-start | bytes 1769476
  7.2 90.6 %all-gather.6.cloned.1.call-start = ((), (), s32[]{:S(2)}) async-start(), calls=%async_computation.6 | async-start | bytes 1769472 | tf_op jit(solution)/shard_map/all_gather | solution.py:43
  7.2 102.6 %collective-permute-start = (bf16[96,768]{1,0:T(8,128)(2,1)}, bf16[96,768]{1,0:T(8,128)(2,1)}, u32[]{:S(2)}, u32[]{:S(2)}) collective-permute-start(bf16[96,768]{1,0:T(8,128)(2,1)} %param.21), channel_id=1, source_target_pairs={{0,1},{1,2},{2,3},{3,4},{4,5},{5,6},{6,7},{7,0},{8,9},{9,10},{10,1... | collective-permute-start | bytes 442376 | tf_op jit(solution)/shard_map/ppermute | solution.py:112
  10.3 99.5 %collective-permute-start.1 = (bf16[96,768]{1,0:T(8,128)(2,1)}, bf16[96,768]{1,0:T(8,128)(2,1)}, u32[]{:S(2)}, u32[]{:S(2)}) collective-permute-start(bf16[96,768]{1,0:T(8,128)(2,1)} %param.21), channel_id=1, source_target_pairs={{0,7},{1,0},{2,1},{3,2},{4,3},{5,4},{6,5},{7,6},{8,15},{9,8},{10,9... | collective-permute-start | bytes 442376 | tf_op jit(solution)/shard_map/ppermute | solution.py:113
  13.4 3.1 copy-start.11
  21.5 5.9 %copy-start.30 = (u32[32]{0:T(128)S(1)}, u32[32]{0:T(128)}, u32[]{:S(2)}) copy-start(u32[32]{0:T(128)} %constant.79) | copy-start | bytes 388
  21.5 7.1 %copy-start.33 = (bf16[288]{0:T(512)(128)(2,1)S(1)}, bf16[288]{0:T(512)(128)(2,1)}, u32[]{:S(2)}) copy-start(bf16[288]{0:T(512)(128)(2,1)} %param.20) | copy-start | bytes 1732
  21.5 7.1 %copy-start.36 = (bf16[96]{0:T(256)(128)(2,1)S(1)}, bf16[96]{0:T(256)(128)(2,1)}, u32[]{:S(2)}) copy-start(bf16[96]{0:T(256)(128)(2,1)} %param.15) | copy-start | bytes 580
  21.5 7.1 %copy-start.37 = (bf16[96]{0:T(256)(128)(2,1)S(1)}, bf16[96]{0:T(256)(128)(2,1)}, u32[]{:S(2)}) copy-start(bf16[96]{0:T(256)(128)(2,1)} %param.16) | copy-start | bytes 580
  21.5 7.1 %copy-start.38 = (bf16[96]{0:T(256)(128)(2,1)S(1)}, bf16[96]{0:T(256)(128)(2,1)}, u32[]{:S(2)}) copy-start(bf16[96]{0:T(256)(128)(2,1)} %param.17) | copy-start | bytes 580
  21.5 7.1 %copy-start.39 = (bf16[96]{0:T(256)(128)(2,1)S(1)}, bf16[96]{0:T(256)(128)(2,1)}, u32[]{:S(2)}) copy-start(bf16[96]{0:T(256)(128)(2,1)} %param.18) | copy-start | bytes 580
  21.5 7.1 %copy-start.40 = (bf16[96]{0:T(256)(128)(2,1)S(1)}, bf16[96]{0:T(256)(128)(2,1)}, u32[]{:S(2)}) copy-start(bf16[96]{0:T(256)(128)(2,1)} %param.22) | copy-start | bytes 580
  21.5 7.1 %copy-start.41 = (bf16[96]{0:T(256)(128)(2,1)S(1)}, bf16[96]{0:T(256)(128)(2,1)}, u32[]{:S(2)}) copy-start(bf16[96]{0:T(256)(128)(2,1)} %param.26) | copy-start | bytes 580
  21.6 73.3 %copy-start.32 = (bf16[384]{0:T(512)(128)(2,1)S(1)}, bf16[384]{0:T(512)(128)(2,1)}, u32[]{:S(2)}) copy-start(bf16[384]{0:T(512)(128)(2,1)} %param.24) | copy-start | bytes 2308
  22.3 78.1 %all-to-all-start = ((bf16[8,96,768]{2,1,0:T(8,128)(2,1)}), bf16[8,96,768]{2,1,0:T(8,128)(2,1)}, u32[]{:S(2)}, u32[]{:S(2)}) async-start(bf16[8,96,768]{2,1,0:T(8,128)(2,1)} %fusion.81), calls=%async_computation | async-start | bytes 2359296 | tf_op jit(solution)/shard_map/all_to_all | solution.py:51
  26.5 90.1 %all-gather.8.cloned.1.call-start = ((), (), s32[]{:S(2)}) async-start(), calls=%async_computation.7 | async-start | bytes 1769472 | tf_op jit(solution)/shard_map/all_gather | solution.py:43
  27.3 177.7 %all-reduce.5.cloned.1.call-start = ((), (), s32[]{:S(2)}) async-start(), calls=%async_computation.8 | async-start | bytes 3833856 | tf_op jit(solution)/shard_map/psum | solution.py:55
  94.6 5.8 %copy-start.24 = (f32[768]{0:T(1024)}, f32[768]{0:T(1024)S(1)}, u32[]{:S(2)}) copy-start(f32[768]{0:T(1024)S(1)} %add.154) | copy-start | bytes 9220
  94.7 5.7 %copy-start.26 = (f32[768]{0:T(1024)}, f32[768]{0:T(1024)S(1)}, u32[]{:S(2)}) copy-start(f32[768]{0:T(1024)S(1)} %mul.430) | copy-start | bytes 9220
  95.5 4.9 %copy-start.28 = (pred[128]{0:T(512)(128)(4,1)}, pred[128]{0:T(512)(128)(4,1)S(1)}, u32[]{:S(2)}) copy-start(pred[128]{0:T(512)(128)(4,1)S(1)} %compare_and_fusion) | copy-start | bytes 388
  97.8 1.9 copy-start.1
  103.4 0.8 copy-start.20
  103.5 2.4 copy-start.8
  104.2 1.7 copy-start.13
  104.2 1.7 copy-start.17
  105.9 3.3 copy-start.4
  116.6 2.2 copy-start.15
  116.6 2.2 copy-start.23
  118.8 6.5 %copy-start.5 = (f32[2,1024,1024]{1,2,0:T(8,128)S(1)}, f32[2,1024,1024]{1,2,0:T(8,128)}, u32[]{:S(2)}) copy-start(f32[2,1024,1024]{1,2,0:T(8,128)} %copy-done.4) | copy-start | bytes 25165828
  125.3 3.3 copy-start.18
  128.6 1.0 copy-start.9
  128.6 1.0 copy-start.14
  131.0 2.5 copy-start.19
  133.4 0.7 copy-start.29
  135.3 0.7 copy-start.31
  136.0 2.3 copy-start.2
  141.7 1.9 copy-start.35
  143.5 0.7 copy-start.25
  143.5 0.7 copy-start.27
  151.6 2.2 copy-start.12
  153.9 1.8 copy-start.3
  157.9 142.4 %reduce-scatter.5.cloned.1.call-start = ((), (), s32[]{:S(2)}) async-start(), calls=%async_computation.5 | async-start | bytes 1769472 | tf_op jit(solution)/shard_map/reduce_scatter | solution.py:47
  158.4 52.1 %copy-start.22 = (f32[8,96]{1,0:T(8,128)S(1)}, f32[8,96]{1,0:T(8,128)}, u32[]{:S(2)}) copy-start(f32[8,96]{1,0:T(8,128)} %get-tuple-element.100) | copy-start | bytes 9220
  158.4 52.2 %copy-start.21 = (f32[8,96]{1,0:T(8,128)S(1)}, f32[8,96]{1,0:T(8,128)}, u32[]{:S(2)}) copy-start(f32[8,96]{1,0:T(8,128)} %get-tuple-element.101) | copy-start | bytes 9220
  158.5 52.3 %copy-start.6 = (bf16[1,128,768]{2,1,0:T(8,128)(2,1)S(1)}, bf16[1,128,768]{2,1,0:T(8,128)(2,1)}, u32[]{:S(2)}) copy-start(bf16[1,128,768]{2,1,0:T(8,128)(2,1)} %param.14) | copy-start | bytes 589828
  205.0 84.9 %all-to-all-start.1 = ((bf16[8,96,768]{2,1,0:T(8,128)(2,1)}), bf16[8,96,768]{2,1,0:T(8,128)(2,1)}, u32[]{:S(2)}, u32[]{:S(2)}) async-start(bf16[8,96,768]{2,1,0:T(8,128)(2,1)} %get-tuple-element.20), calls=%async_computation.3 | async-start | bytes 2359296 | tf_op jit(solution)/shard_map/all_to_all | solution.py:57
  210.5 142.1 %reduce-scatter.3.cloned.1.call-start = ((), (), s32[]{:S(2)}) async-start(), calls=%async_computation.4 | async-start | bytes 1769472 | tf_op jit(solution)/shard_map/reduce_scatter | solution.py:47
  283.3 1.0 copy-start.16
  283.3 1.0 copy-start.34
  287.0 1.1 copy-start.7
  294.9 57.7 %copy-start.10 = (bf16[1,128,768]{2,1,0:T(8,128)(2,1)S(1)}, bf16[1,128,768]{2,1,0:T(8,128)(2,1)}, u32[]{:S(2)}) copy-start(bf16[1,128,768]{2,1,0:T(8,128)(2,1)} %param.27) | copy-start | bytes 589828
  296.9 57.7 %copy-start.42 = (f32[96]{0:T(128)S(1)}, f32[96]{0:T(128)}, u32[]{:S(2)}) copy-start(f32[96]{0:T(128)} %get-tuple-element.175) | copy-start | bytes 1156
Sparse Core Ops, SparseCore 0:
  13.5 57.5 all-gather.5
  73.3 43.2 all-gather.7
  158.0 46.9 all-reduce.4
  208.3 76.4 reduce-scatter.4
  288.0 64.5 reduce-scatter.2

commit v2 on v1

--- a/solution.py
+++ b/solution.py
@@ -44,7 +44,9 @@
 
 
 def scatter_rows(a):
-    return lax.psum_scatter(a, "fsdp", scatter_dimension=0, tiled=True)
+    F = lax.axis_size("fsdp")
+    got = lax.all_to_all(a, "fsdp", 0, 0, tiled=True)
+    return jnp.sum(got.reshape((F, a.shape[0] // F) + a.shape[1:]).astype(f32), axis=0)
 
 
 def spread_weights(blocks):
@@ -52,9 +54,28 @@
 
 
 def return_grads(blocks, own):
-    summed = lax.psum(blocks, "dp")
-    own = lax.psum(own, "dp")
-    return lax.all_to_all(summed, "fsdp", 0, 0, tiled=True), own
+    n = lax.axis_size("dp")
+    F, W, C = blocks.shape
+    R, D = own.shape
+    parts = jnp.swapaxes(blocks.reshape(F, n, W // n, C), 0, 1).reshape(n, F * (W // n), C)
+    own_parts = own.reshape(n, R // n, D)
+    if C == D:
+        both = jnp.concatenate([parts, own_parts], axis=1)
+        both = jnp.sum(lax.all_to_all(both, "dp", 0, 0, tiled=True).astype(f32), axis=0)
+        part, own_part = both[: F * (W // n)].astype(bf16), both[F * (W // n) :].astype(bf16)
+    else:
+        part = jnp.sum(lax.all_to_all(parts, "dp", 0, 0, tiled=True).astype(f32), axis=0)
+        own_part = jnp.sum(lax.all_to_all(own_parts, "dp", 0, 0, tiled=True).astype(f32), axis=0)
+        part, own_part = part.astype(bf16), own_part.astype(bf16)
+    part = lax.all_to_all(part, "fsdp", 0, 0, tiled=True)
+    if C == D:
+        whole = lax.all_gather(jnp.concatenate([part, own_part], axis=0), "dp", axis=0)
+        part_all, own_all = whole[:, : F * (W // n)], whole[:, F * (W // n) :]
+    else:
+        part_all = lax.all_gather(part, "dp", axis=0)
+        own_all = lax.all_gather(own_part, "dp", axis=0)
+    part_all = jnp.swapaxes(part_all.reshape(n, F, W // n, C), 0, 1).reshape(F, W, C)
+    return part_all, own_all.reshape(R, D)
 
 
 def body(
@@ -102,8 +123,13 @@
     )
     smalls = jnp.concatenate(
         [ln1_gain, ln1_bias, ln2_gain, ln2_bias, out_bias, down_bias, qkv_bias]
-    )[None]
-    x_low, small_all = gather_rows([tokens[0], smalls])
+    )
+    extra = -(-smalls.shape[0] // (16 * D)) * 16
+    smalls = jnp.concatenate([smalls, jnp.zeros(extra * D - smalls.shape[0], bf16)])
+    (both_all,) = gather_rows([jnp.concatenate([tokens[0], smalls.reshape(extra, D)], axis=0)])
+    both_all = both_all.reshape(F, rows + extra, D)
+    x_low = both_all[:, :rows].reshape(S, D)
+    small_all = both_all[:, rows:].reshape(F, extra * D)
     wall = spread_weights(blocks).reshape(D, 3 * WIN + FFW)
     w_qkv = wall[:, : 3 * WIN]
     w_up = wall[:, 3 * WIN :]
@@ -122,7 +148,7 @@
     gain_one, bias_one, gain_two, bias_two, b_out, b_down = [
         small_all[:, i * W : (i + 1) * W].reshape(D) for i in range(6)
     ]
-    b_qkv = small_all[:, 6 * W :].reshape(3, D)
+    b_qkv = small_all[:, 6 * W : 9 * W].reshape(3, D)
     b_qkv = lax.dynamic_slice_in_dim(b_qkv, start, WIN, 1).reshape(3 * WIN)
     b_up = up_bias.astype(f32)
 
@@ -159,7 +185,7 @@
     cdf = 0.5 * (1.0 + lax.erf(hidden_pre * inv_root_two))
     hidden_low = (hidden_pre * cdf).astype(bf16)
     part = dot(att_low, w_out_win, NN) + dot(hidden_low, down_weight, NN)
-    branch = scatter_rows(part.astype(bf16)).astype(f32)
+    branch = scatter_rows(part.astype(bf16))
 
     grad_hidden = dot(grad_out, down_weight, NT)
     slope = cdf + hidden_pre * jnp.exp(-0.5 * hidden_pre * hidden_pre) * inv_root_twopi
@@ -201,19 +227,25 @@
     small_part = jnp.concatenate(
         [v.reshape(F, W) for v in vectors] + [b_full.reshape(F, 3 * W)], axis=1
     )
-    mixed_mine = scatter_rows(mixed.astype(bf16)).astype(f32)
+    mixed_mine = scatter_rows(mixed.astype(bf16))
     small_mine = scatter_rows(small_part)[0]
     own_small = jnp.concatenate(
         [small_mine, lax.dynamic_slice_in_dim(bias_total, rank * W, W, 0), grad_b_up]
     )
-    own_small = lax.psum(own_small, "dp")
+    pad = 8 * lax.axis_size("dp")
+    own_rows = -(-(W + FFW + -(-own_small.shape[0] // D)) // pad) * pad
+    n_small = own_rows - W - FFW
+    own_small = jnp.concatenate([own_small, jnp.zeros(n_small * D - own_small.shape[0], f32)])
 
     grad_blocks = jnp.concatenate([grad_w_qkv, grad_w_up], axis=1).astype(bf16)
     grad_blocks = grad_blocks.reshape(F, W, 3 * WIN + FFW)
-    own = jnp.concatenate([grad_w_out, grad_w_down], axis=0).astype(bf16)
+    own = jnp.concatenate(
+        [grad_w_out, grad_w_down, own_small.reshape(n_small, D)], axis=0
+    ).astype(bf16)
     returned, own = return_grads(grad_blocks, own)
     returned = returned.astype(f32)
     own = own.astype(f32)
+    own_small = own[W + FFW :].reshape(n_small * D)
     pieces = [
         [returned[g, :, i * WIN + g * W - s : i * WIN + g * W - s + W] for g, s in enumerate(starts)]
         for i in range(3)
@@ -246,8 +278,8 @@
         own[:W],
         bias_mine,
         out_w_up,
-        own_small[8 * W :],
-        own[W:],
+        own_small[8 * W : 8 * W + FFW],
+        own[W : W + FFW],
         bias_mine,
     )
 

time: 363 us -> 342 us (0.942)
  blocking collectives: 134 us -> 43.1 us
  waiting for transfers between devices: 106 us -> 146 us
  local copies, waits for them, and re-layouts: 28.3 us -> 45.6 us
  other arithmetic: 22.5 us -> 29.7 us
  starting transfers between devices: 16.1 us -> 22.9 us
    unnamed x2 -> x0, blocking collectives: 128 us -> none
    all_gather x2, waiting for transfers between devices: 6.78 us -> 79 us  [gather_rows(): return [lax.all_gather(a, 'fsdp', axis=0, tiled=True) for a in arrays]]
    all_to_all x1 -> x3, waiting for transfers between devices: 0.01 us -> 66.6 us  [scatter_rows(): got = lax.all_to_all(a, 'fsdp', 0, 0, tiled=True)]
    reduce_scatter x2 -> x0, waiting for transfers between devices: 51.2 us -> none  [scatter_rows(): return lax.psum_scatter(a, 'fsdp', scatter_dimension=0, tiled=True)]
    psum x1 -> x0, waiting for transfers between devices: 46.5 us -> none  [return_grads(): summed = lax.psum(blocks, 'dp')]
    all_to_all x0 -> x2, blocking collectives: none -> 43.1 us  [the longest x1 27.5 us: return_grads(): lax.all_to_all(both, 'dp', 0, 0, tiled=True).astype(f32)]
    concatenate x2, local copies, waits for them, and re-layouts: 0.16 us -> 8.32 us  [the longest x1 4.79 us: body(): jnp.concatenate([smalls, jnp.zeros(extra * D - smalls.shape[0], bf16)])]
    all_to_all x1 -> x3, starting transfers between devices: 5.52 us -> 12.2 us  [scatter_rows(): got = lax.all_to_all(a, 'fsdp', 0, 0, tiled=True)]
  transfers between devices with their start and end apart: 9 -> 9, of which waited for: 3 -> 4; matrix products, arithmetic and copies ran while one was open for 12% -> 15% of each run, Pallas kernels for 0% -> 0%
where the time goes in v2:
time: 342 us; the launch traced here: 340 us
  waiting for transfers between devices  146 us (43%)
  local copies, waits for them, and re-layouts  45.6 us (13%)
  blocking collectives  43.1 us (13%)
  matrix products  38.3 us (11%)
  other arithmetic  29.7 us (9%)
  starting transfers between devices  22.9 us (7%)
  between operations  14.6 us (4%)
    all_gather x2, waiting for transfers between devices, gather_rows(): return [lax.all_gather(a, 'fsdp', axis=0, tiled=True) for a in arrays]  79 us
    all_to_all x3, waiting for transfers between devices, scatter_rows(): got = lax.all_to_all(a, 'fsdp', 0, 0, tiled=True)  66.6 us
    all_to_all x1, blocking collectives, return_grads(): lax.all_to_all(both, 'dp', 0, 0, tiled=True).astype(f32)  27.5 us
    dot_general x12, matrix products, dot(): lax.dot_general(a, b, ((dims[0], dims[1]), ((), ())), preferred_element_t...  26.3 us
    all_to_all x1, blocking collectives, return_grads(): part = lax.all_to_all(part, 'fsdp', 0, 0, tiled=True)  15.6 us
    unnamed x72, local copies, waits for them, and re-layouts  14.3 us
    all_to_all x3, starting transfers between devices, scatter_rows(): got = lax.all_to_all(a, 'fsdp', 0, 0, tiled=True)  12.2 us
  transfers between devices with their start and end apart: 9, of which 4 were waited for; matrix products, arithmetic and copies ran while one was open for 15% of the time, Pallas kernels for 0%

profile of v2, /device:TPU:0, one launch (start us, length us, event | category | flops | bytes accessed | tf_op | source)
XLA Modules:
  0.0 340.4 jit_solution(5469213770483834597)
XLA Ops:
  8.0 3.0 collective-permute-start
  11.0 3.1 collective-permute-start.1
  14.1 4.8 %concatenate.74 = bf16[12288]{0:T(1024)(128)(2,1)S(1)} concatenate(bf16[96]{0:T(256)(128)(2,1)} %param.15, bf16[96]{0:T(256)(128)(2,1)} %param.16, bf16[96]{0:T(256)(128)(2,1)} %param.17, bf16[96]{0:T(256)(128)(2,1)} %param.18, bf16[96]{0:T(256)(128)(2,1)} %param.22, bf16[96]{0:T(256)(128)(2,1)} %param.26, bf16[288]{0:T(512)(128)(2,1)} %param.20, ...), dimensions={0} | concatenate | bytes 49152 | tf_op jit(solution)/shard_map/concatenate | solution.py:128
  19.0 1.6 pad_maximum_fusion.7
  20.7 1.6 reshape.377
  22.6 1.1 fusion.88
  29.4 4.4 %all-to-all-start = ((bf16[8,96,768]{2,1,0:T(8,128)(2,1)}), bf16[8,96,768]{2,1,0:T(8,128)(2,1)}, u32[]{:S(2)}, u32[]{:S(2)}) async-start(bf16[8,96,768]{2,1,0:T(8,128)(2,1)} %fusion.67), calls=%async_computation | async-start | bytes 2359296 | tf_op jit(solution)/shard_map/all_to_all | solution.py:53
  35.0 37.7 %all-gather.8.cloned.1.call-done = bf16[1,1024,768]{2,1,0:T(8,128)(2,1)} async-done(((bf16[1,128,768]{2,1,0:T(8,128)(2,1)}), bf16[1,1024,768]{2,1,0:T(8,128)(2,1)}) %all-gather.8.cloned.1.call-update) | async-done | bytes 1572880 | tf_op jit(solution)/shard_map/all_gather | solution.py:43
  72.7 1.8 convert_reduce_fusion.2
  75.2 2.2 fusion.23
  77.3 41.3 %all-gather.6.cloned.1.call-done = bf16[1152,768]{1,0:T(8,128)(2,1)} async-done(((bf16[144,768]{1,0:T(8,128)(2,1)}), bf16[1152,768]{1,0:T(8,128)(2,1)}) %all-gather.6.cloned.1.call-update) | async-done | bytes 1769488 | tf_op jit(solution)/shard_map/all_gather | solution.py:43
  118.6 1.1 convert_bitcast_fusion
  121.1 1.7 convert_reduce_fusion.4
  123.4 2.6 add_convert_fusion.4
  126.0 2.4 convolution_add_fusion.1
  128.6 1.7 select_reduce_fusion
  130.3 1.7 exponential_reduce_fusion
  132.0 2.4 fusion.69
  134.4 2.4 fusion.29
  136.8 3.3 multiply_convert_fusion
  140.1 1.4 convolution_bitcast_fusion
  141.5 0.8 fusion.22
  142.6 1.1 convert_reduce_fusion.5
  144.0 2.2 fusion.33
  146.3 2.3 multiply_convert_fusion.1
  148.6 1.9 fusion.93
  150.5 4.1 %fusion.85 = (f32[768]{0:T(1024)S(1)}, f32[768]{0:T(1024)S(1)}, bf16[1024,768]{1,0:T(8,128)(2,1)}, f32[768]{0:T(1024)S(1)}, f32[768]{0:T(1024)S(1)}) fusion(f32[1024]{0:T(1024)S(1)} %get-tuple-element.111, f32[1024]{0:T(1024)S(1)} %get-tuple-element.112, bf16[8,144,768]{2,1,0:T(8,128)(2,1)S(1)} %bitcast.299, f32[768]{0:T(1024)S(1)} %mul.466, ...), kind=kOutput, calls=%fused_computation.216 | convolution fusion | flops 614200320 | bytes 7694336 | tf_op jit(solution)/shard_map/dot_general | solution.py:34
  155.9 4.2 %all-to-all-start.3 = ((f32[8,1,672]{2,1,0:T(1,128)}), f32[8,1,672]{2,1,0:T(1,128)}, u32[]{:S(2)}, u32[]{:S(2)}) async-start(f32[8,1,672]{2,1,0:T(1,128)} %all_to_all.37), calls=%async_computation.3 | async-start | bytes 49152 | tf_op jit(solution)/shard_map/all_to_all | solution.py:48
  160.1 2.6 copy.64
  162.7 3.4 convolution_convert_fusion
  166.1 1.8 add_convert_fusion
  167.9 1.7 copy.62
  169.7 2.2 convolution_convert_fusion.1
  172.0 1.3 copy-done.4
  173.3 1.6 fusion.19
  175.4 1.4 reduce_sum.192
  177.4 3.5 %concatenate.91 = bf16[24576]{0:T(1024)(128)(2,1)} concatenate(bf16[672]{0:T(1024)(128)(2,1)} %reduce_sum.192, bf16[96]{0:T(256)(128)(2,1)} %dynamic_slice.41, bf16[384]{0:T(512)(128)(2,1)} %get-tuple-element.123, bf16[23424]{0:T(1024)(128)(2,1)} %broadcast_in_dim.80), dimensions={0} | concatenate | bytes 98304 | tf_op jit(solution)/shard_map/concatenate | solution.py:238
  181.0 1.5 reshape.391
  182.5 0.8 pad_maximum_fusion.2
  183.4 27.5 %all_to_all.49 = bf16[4,320,768]{2,1,0:T(8,128)(2,1)} all-to-all(bf16[4,320,768]{2,1,0:T(8,128)(2,1)S(1)} %pad_maximum_fusion), channel_id=1, replica_groups=mesh['dp'=4,'fsdp'=8] {'dp'}, dimensions={0} | all-to-all | bytes 3932160 | tf_op jit(solution)/shard_map/all_to_all | solution.py:64
  210.9 2.1 reduce.13
  213.0 15.6 %all_to_all.50 = bf16[8,24,768]{2,1,0:T(8,128)(2,1)} all-to-all(bf16[8,24,768]{2,1,0:T(8,128)(2,1)S(1)} %bitcast.331), channel_id=1, replica_groups=mesh['dp'=4,'fsdp'=8] {'fsdp'}, dimensions={0} | all-to-all | bytes 589824 | tf_op jit(solution)/shard_map/all_to_all | solution.py:70
  228.6 3.6 %all-to-all-start.2 = ((bf16[8,128,768]{2,1,0:T(8,128)(2,1)}), bf16[8,128,768]{2,1,0:T(8,128)(2,1)S(1)}, u32[]{:S(2)}, u32[]{:S(2)}) async-start(bf16[8,128,768]{2,1,0:T(8,128)(2,1)} %bitcast.326), calls=%async_computation.2 | async-start | bytes 3145728 | tf_op jit(solution)/shard_map/all_to_all | solution.py:48
  232.2 1.0 fusion.94
  233.2 2.7 add_convert_fusion.2
  235.9 32.3 %all-to-all-done.2 = bf16[8,128,768]{2,1,0:T(8,128)(2,1)S(1)} async-done(((bf16[8,128,768]{2,1,0:T(8,128)(2,1)}), bf16[8,128,768]{2,1,0:T(8,128)(2,1)S(1)}, u32[]{:S(2)}, u32[]{:S(2)}) %all-to-all-start.2) | async-done | bytes 1572896 | tf_op jit(solution)/shard_map/all_to_all | solution.py:48
  268.2 4.4 %all-to-all-start.1 = ((bf16[8,128,768]{2,1,0:T(8,128)(2,1)}), bf16[8,128,768]{2,1,0:T(8,128)(2,1)}, u32[]{:S(2)}, u32[]{:S(2)}) async-start(bf16[8,128,768]{2,1,0:T(8,128)(2,1)} %bitcast.313), calls=%async_computation.1 | async-start | bytes 3145728 | tf_op jit(solution)/shard_map/all_to_all | solution.py:48
  272.7 0.8 pad_maximum_fusion.5
  274.7 34.3 %all-to-all-done.1 = bf16[8,128,768]{2,1,0:T(8,128)(2,1)} async-done(((bf16[8,128,768]{2,1,0:T(8,128)(2,1)}), bf16[8,128,768]{2,1,0:T(8,128)(2,1)}, u32[]{:S(2)}, u32[]{:S(2)}) %all-to-all-start.1) | async-done | bytes 1572896 | tf_op jit(solution)/shard_map/all_to_all | solution.py:48
  309.0 1.7 convert_reduce_fusion.3
  310.7 1.0 fusion.48
  311.7 1.2 slice.472
  312.9 1.4 slice.478
  314.9 1.0 copy-done.5
  317.8 1.6 fusion.59
  320.0 1.1 slice.515
  321.1 1.6 fusion.58
  322.7 1.6 fusion.57
  324.2 1.6 fusion.56
  325.8 1.6 fusion.55
  327.4 1.6 fusion.54
  329.0 1.6 fusion.53
  330.6 1.6 fusion.52
  332.1 1.2 concatenate.95
  (158 shorter events, 18.7 us)
Async XLA Ops:
  7.2 141.4 %copy-start = (bf16[384,768]{1,0:T(8,128)(2,1)S(1)}, bf16[384,768]{1,0:T(8,128)(2,1)}, u32[]{:S(2)}) copy-start(bf16[384,768]{1,0:T(8,128)(2,1)} %param.25) | copy-start | bytes 1769476
  7.2 65.6 %all-gather.8.cloned.1.call-start = ((), (), s32[]{:S(2)}) async-start(), calls=%async_computation.7 | async-start | bytes 1769472 | tf_op jit(solution)/shard_map/all_gather | solution.py:43
  7.9 110.7 %all-gather.6.cloned.1.call-start = ((), (), s32[]{:S(2)}) async-start(), calls=%async_computation.6 | async-start | bytes 1990656 | tf_op jit(solution)/shard_map/all_gather | solution.py:43
  8.0 67.2 %collective-permute-start = (bf16[96,768]{1,0:T(8,128)(2,1)}, bf16[96,768]{1,0:T(8,128)(2,1)}, u32[]{:S(2)}, u32[]{:S(2)}) collective-permute-start(bf16[96,768]{1,0:T(8,128)(2,1)} %param.21), channel_id=1, source_target_pairs={{0,1},{1,2},{2,3},{3,4},{4,5},{5,6},{6,7},{7,0},{8,9},{9,10},{10,1... | collective-permute-start | bytes 442376 | tf_op jit(solution)/shard_map/ppermute | solution.py:138
  11.0 64.1 %collective-permute-start.1 = (bf16[96,768]{1,0:T(8,128)(2,1)}, bf16[96,768]{1,0:T(8,128)(2,1)}, u32[]{:S(2)}, u32[]{:S(2)}) collective-permute-start(bf16[96,768]{1,0:T(8,128)(2,1)} %param.21), channel_id=1, source_target_pairs={{0,7},{1,0},{2,1},{3,2},{4,3},{5,4},{6,5},{7,6},{8,15},{9,8},{10,9... | collective-permute-start | bytes 442376 | tf_op jit(solution)/shard_map/ppermute | solution.py:139
  20.6 3.0 copy-start.12
  28.0 5.9 %copy-start.18 = (bf16[384]{0:T(512)(128)(2,1)S(1)}, bf16[384]{0:T(512)(128)(2,1)}, u32[]{:S(2)}) copy-start(bf16[384]{0:T(512)(128)(2,1)} %param.24) | copy-start | bytes 2308
  29.4 96.6 %all-to-all-start = ((bf16[8,96,768]{2,1,0:T(8,128)(2,1)}), bf16[8,96,768]{2,1,0:T(8,128)(2,1)}, u32[]{:S(2)}, u32[]{:S(2)}) async-start(bf16[8,96,768]{2,1,0:T(8,128)(2,1)} %fusion.67), calls=%async_computation | async-start | bytes 2359296 | tf_op jit(solution)/shard_map/all_to_all | solution.py:53
  33.8 41.4 %copy-start.14 = (bf16[96,768]{1,0:T(8,128)(2,1)S(1)}, bf16[96,768]{1,0:T(8,128)(2,1)}, u32[]{:S(2)}) copy-start(bf16[96,768]{1,0:T(8,128)(2,1)} %param.21) | copy-start | bytes 442372
  34.0 43.3 %copy-start.19 = (bf16[128]{0:T(256)(128)(2,1)}, bf16[128]{0:T(256)(128)(2,1)S(1)}, u32[]{:S(2)}) copy-start(bf16[128]{0:T(256)(128)(2,1)S(1)} %pad_dynamic-slice_fusion.3) | copy-start | bytes 772
  72.7 2.4 copy-start.2
  118.6 4.2 %copy-start.1 = (bf16[1152,768]{1,0:T(8,128)(2,1)S(1)}, bf16[1152,768]{1,0:T(8,128)(2,1)}, u32[]{:S(2)}) copy-start(bf16[1152,768]{1,0:T(8,128)(2,1)} %all-gather.6.cloned.1.call-done) | copy-start | bytes 5308420
  130.3 1.8 copy-start.23
  142.5 1.2 copy-start.21
  143.9 2.3 copy-start.6
  146.3 2.3 copy-start.3
  150.5 4.1 %copy-start.24 = (bf16[1024,384]{1,0:T(8,128)(2,1)}, bf16[1024,384]{1,0:T(8,128)(2,1)S(1)}, u32[]{:S(2)}) copy-start(bf16[1024,384]{1,0:T(8,128)(2,1)S(1)} %get-tuple-element.124) | copy-start | bytes 2359300
  155.9 19.6 %all-to-all-start.3 = ((f32[8,1,672]{2,1,0:T(1,128)}), f32[8,1,672]{2,1,0:T(1,128)}, u32[]{:S(2)}, u32[]{:S(2)}) async-start(f32[8,1,672]{2,1,0:T(1,128)} %all_to_all.37), calls=%async_computation.3 | async-start | bytes 49152 | tf_op jit(solution)/shard_map/all_to_all | solution.py:48
  169.6 2.2 copy-start.13
  171.9 1.4 copy-start.4
  175.3 7.2 %copy-start.8 = (bf16[384,768]{1,0:T(8,128)(2,1)S(1)}, bf16[384,768]{1,0:T(8,128)(2,1)}, u32[]{:S(2)}) copy-start(bf16[384,768]{1,0:T(8,128)(2,1)} %fusion.19) | copy-start | bytes 1769476
  213.0 15.6 %copy-start.9 = (bf16[320,768]{1,0:T(8,128)(2,1)}, bf16[320,768]{1,0:T(8,128)(2,1)S(1)}, u32[]{:S(2)}) copy-start(bf16[320,768]{1,0:T(8,128)(2,1)S(1)} %reduce.13) | copy-start | bytes 1474564
  228.6 39.6 %all-to-all-start.2 = ((bf16[8,128,768]{2,1,0:T(8,128)(2,1)}), bf16[8,128,768]{2,1,0:T(8,128)(2,1)S(1)}, u32[]{:S(2)}, u32[]{:S(2)}) async-start(bf16[8,128,768]{2,1,0:T(8,128)(2,1)} %bitcast.326), calls=%async_computation.2 | async-start | bytes 3145728 | tf_op jit(solution)/shard_map/all_to_all | solution.py:48
  232.2 1.0 copy-start.15
  232.2 1.0 copy-start.20
  268.2 4.5 %slice-start = ((bf16[320,768]{1,0:T(8,128)(2,1)}), bf16[128,768]{1,0:T(8,128)(2,1)S(1)}, s32[]{:S(2)}) async-start(bf16[320,768]{1,0:T(8,128)(2,1)} %copy-done.9), calls=%async_computation.9 | async-start | bytes 393216 | tf_op jit(solution)/shard_map/slice | solution.py:65
  268.2 4.5 %copy-start.10 = (bf16[8,24,768]{2,1,0:T(8,128)(2,1)S(1)}, bf16[8,24,768]{2,1,0:T(8,128)(2,1)}, u32[]{:S(2)}) copy-start(bf16[8,24,768]{2,1,0:T(8,128)(2,1)} %all_to_all.50) | copy-start | bytes 884740
  268.2 40.8 %all-to-all-start.1 = ((bf16[8,128,768]{2,1,0:T(8,128)(2,1)}), bf16[8,128,768]{2,1,0:T(8,128)(2,1)}, u32[]{:S(2)}, u32[]{:S(2)}) async-start(bf16[8,128,768]{2,1,0:T(8,128)(2,1)} %bitcast.313), calls=%async_computation.1 | async-start | bytes 3145728 | tf_op jit(solution)/shard_map/all_to_all | solution.py:48
  272.6 0.9 copy-start.7
  272.6 1.3 copy-start.17
  272.6 1.4 copy-start.16
  272.7 39.0 %all-gather.10.cloned.1.call-start = ((), (), s32[]{:S(2)}) async-start(), calls=%async_computation.8 | async-start | bytes 2457600 | tf_op jit(solution)/shard_map/all_gather | solution.py:72
  274.5 36.2 %copy-start.11 = (bf16[1,128,768]{2,1,0:T(8,128)(2,1)S(1)}, bf16[1,128,768]{2,1,0:T(8,128)(2,1)}, u32[]{:S(2)}) copy-start(bf16[1,128,768]{2,1,0:T(8,128)(2,1)} %param.27) | copy-start | bytes 589828
  314.5 1.4 copy-start.5
  316.5 16.8 %copy-start.22 = (f32[96]{0:T(128)}, f32[96]{0:T(128)S(1)}, u32[]{:S(2)}) copy-start(f32[96]{0:T(128)S(1)} %get-tuple-element.176) | copy-start | bytes 1156
Sparse Core Ops, SparseCore 0:
  10.2 62.5 all-gather.7
  75.5 43.0 all-gather.5
  275.6 22.6 all-gather.9
